TPU v7x, 128 devices: a whole 4x4x4 slice. The times are simulated.
128 devices in a mesh: neuron: 16 (over z, y), trial: 8 (over x, core).
Axes of the slice: x: 4, y: 4, z: 4, core: 2. Of those that a mesh axis runs over, the one named last changes fastest.
Arguments:
- drive: bfloat16 [8, 128, 131072], P(None, 'trial', 'neuron'), may hold values from -6 to 6
- learning: bfloat16 [8, 128, 131072], P(None, 'trial', 'neuron'), may hold values from -6 to 6
- membrane_init: float32 [128, 131072], P('trial', 'neuron'), may hold values from -3 to 3
- adapt_init: float32 [128, 131072], P('trial', 'neuron'), may hold values from 0 to 1
- trace_init: float32 [128, 131072], P('trial', 'neuron'), may hold values from 0 to 3
- membrane_decay: float32 [131072], P('neuron'), may hold values from 0.6 to 0.95
- adapt_decay: float32 [131072], P('neuron'), may hold values from 0.8 to 0.99
- adapt_gain: float32 [131072], P('neuron'), may hold values from 0.2 to 1
- threshold: float32 [131072], P('neuron'), may hold values from 0.5 to 1.5
- left_factor: bfloat16 [131072, 512], P('neuron'), may hold values from -6 to 6
- right_factor: bfloat16 [131072, 512], P('neuron'), may hold values from -16 to 16
Outputs:
- left_new: bfloat16 [131072, 512], P(('neuron', 'trial'))
- right_new: bfloat16 [131072, 512], P(('neuron', 'trial'))
All inputs are finite; a program needn't handle non-finite values.
Results may differ from a plain program's by a relative error of at most 0.0085.
Values may be sent and summed in bfloat16 or wider, within the bound.
No kernel may reach another device: no remote copies, remote signals or barrier semaphores. Data moves between devices by JAX's collectives and lax.ppermute only.
A program may use at most 128 MiB of HBM per device.

v0:
```python
import math
import jax
import jax.numpy as jnp
from jax import lax
from jax.sharding import PartitionSpec as P

sharpness = 3.0
learn_rate = 0.5


def rank_block(values, factor, weight):
    return jnp.dot(values, factor, preferred_element_type=jnp.float32) * weight


def shards(
    drive,
    learning,
    membrane_init,
    adapt_init,
    trace_init,
    membrane_decay,
    adapt_decay,
    adapt_gain,
    threshold,
    left_factor,
    right_factor,
):
    local_neurons = left_factor.shape[0]
    rank_width = left_factor.shape[1]
    step_count = drive.shape[0]
    neuron_count = local_neurons * lax.axis_size("neuron")
    norm_neurons = 1.0 / math.sqrt(neuron_count)
    norm_rank = 1.0 / math.sqrt(rank_width)
    membrane = membrane_init
    adaptation = adapt_init
    filtered = trace_init
    spikes = jax.nn.sigmoid(sharpness * (membrane - threshold - adapt_gain * adaptation))
    signals = []
    presyns = []
    g_blocks = []
    k_blocks = []
    for moment in range(step_count):
        partial_value = rank_block(spikes.astype(jnp.bfloat16), right_factor, norm_neurons)
        projected = lax.psum(partial_value, "neuron").astype(jnp.bfloat16)
        current = (
            lax.dot_general(
                projected, left_factor, (((1,), (1,)), ((), ())), preferred_element_type=jnp.float32
            )
            * norm_rank
        )
        membrane = (
            membrane_decay * membrane
            + drive[moment].astype(jnp.float32)
            + current
            - threshold * spikes
        )
        adaptation = adapt_decay * adaptation + spikes
        spikes = jax.nn.sigmoid(sharpness * (membrane - threshold - adapt_gain * adaptation))
        slope_value = sharpness * spikes * (1.0 - spikes)
        filtered = membrane_decay * filtered + spikes
        signal = (learning[moment].astype(jnp.float32) * slope_value).astype(jnp.bfloat16)
        presyn = filtered.astype(jnp.bfloat16)
        signals.append(signal)
        presyns.append(presyn)
        g_part = rank_block(presyn, right_factor, norm_neurons)
        k_part = rank_block(signal, left_factor, norm_neurons)
        g_total, k_total = lax.psum((g_part, k_part), "neuron")
        g_blocks.append(g_total.astype(jnp.bfloat16))
        k_blocks.append(k_total.astype(jnp.bfloat16))
    signal_all = jnp.stack(signals)
    presyn_all = jnp.stack(presyns)
    rank_g = jnp.stack(g_blocks)
    rank_k = jnp.stack(k_blocks)
    stored = local_neurons // lax.axis_size("trial")
    offset = lax.axis_index("trial") * stored
    left_rows = lax.dynamic_slice_in_dim(left_factor, offset, stored, 0).astype(jnp.float32)
    right_rows = lax.dynamic_slice_in_dim(right_factor, offset, stored, 0).astype(jnp.float32)
    contract_lead = (((0, 1), (0, 1)), ((), ()))
    signal_mine, presyn_mine = (
        lax.all_to_all(signal_all, "trial", split_axis=2, concat_axis=1, tiled=True),
        lax.all_to_all(presyn_all, "trial", split_axis=2, concat_axis=1, tiled=True),
    )
    first = lax.dot_general(
        signal_mine,
        lax.all_gather(rank_g, "trial", axis=1, tiled=True),
        contract_lead,
        preferred_element_type=jnp.float32,
    )
    second = lax.dot_general(
        presyn_mine,
        lax.all_gather(rank_k, "trial", axis=1, tiled=True),
        contract_lead,
        preferred_element_type=jnp.float32,
    )
    left_step = left_rows - learn_rate * (first * norm_rank)
    right_step = right_rows - learn_rate * (second * norm_rank)
    highest = lax.Precision.HIGHEST
    row_lead = (((0,), (0,)), ((), ()))
    gram_one = lax.psum(
        lax.dot_general(right_step, right_step, row_lead, precision=highest), ("neuron", "trial")
    )
    lower_one = jnp.linalg.cholesky(gram_one)
    basis = lax.linalg.triangular_solve(
        lower_one, right_step, left_side=False, lower=True, transpose_a=True
    )
    right_new = (basis * math.sqrt(neuron_count)).astype(jnp.bfloat16)
    left_new = (jnp.dot(left_step, lower_one, precision=highest) * norm_neurons).astype(
        jnp.bfloat16
    )
    return (left_new, right_new)


def solution(mesh):
    in_specs = (
        P(None, "trial", "neuron"),
        P(None, "trial", "neuron"),
        P("trial", "neuron"),
        P("trial", "neuron"),
        P("trial", "neuron"),
        P("neuron"),
        P("neuron"),
        P("neuron"),
        P("neuron"),
        P("neuron", None),
        P("neuron", None),
    )
    out_specs = (P(("neuron", "trial"), None), P(("neuron", "trial"), None))
    return jax.shard_map(shards, mesh=mesh, in_specs=in_specs, out_specs=out_specs, check_vma=False)
```

profile of v0, /device:TPU:1, one launch (start us, length us, event | category | flops | bytes accessed | tf_op | source)
XLA Modules:
  0.0 1214.8 jit_solution(1713676997602515515)
XLA Ops:
  12.3 62.5 %psum.175 = bf16[16,512]{1,0:T(8,128)(2,1)S(1)} all-reduce(f32[16,512]{1,0:T(8,128)S(1)} %convolution_multiply_fusion.31), channel_id=1, replica_groups=mesh['neuron'=16,'trial'=8] {'neuron'}, use_global_device_ids=true, to_apply=%region_0.0 | all-reduce | flops 8192 | bytes 49152 | tf_op jit(solution)/shard_map/psum | solution.py:44
  82.8 55.9 %psum.176 = bf16[16,512]{1,0:T(8,128)(2,1)S(1)} all-reduce(f32[16,512]{1,0:T(8,128)S(1)} %convolution_multiply_fusion.30), channel_id=1, replica_groups=mesh['neuron'=16,'trial'=8] {'neuron'}, use_global_device_ids=true, to_apply=%region_1.0 | all-reduce | flops 8192 | bytes 49152 | tf_op jit(solution)/shard_map/psum | solution.py:44
  150.7 56.0 %psum.177 = bf16[16,512]{1,0:T(8,128)(2,1)S(1)} all-reduce(f32[16,512]{1,0:T(8,128)S(1)} %convolution_multiply_fusion.29), channel_id=1, replica_groups=mesh['neuron'=16,'trial'=8] {'neuron'}, use_global_device_ids=true, to_apply=%region_2.0 | all-reduce | flops 8192 | bytes 49152 | tf_op jit(solution)/shard_map/psum | solution.py:44
  217.9 55.9 %psum.178 = bf16[16,512]{1,0:T(8,128)(2,1)S(1)} all-reduce(f32[16,512]{1,0:T(8,128)S(1)} %convolution_multiply_fusion.28), channel_id=1, replica_groups=mesh['neuron'=16,'trial'=8] {'neuron'}, use_global_device_ids=true, to_apply=%region_3.0 | all-reduce | flops 8192 | bytes 49152 | tf_op jit(solution)/shard_map/psum | solution.py:44
  273.7 7.1 bitcast_dynamic-update-slice_fusion.5
  287.2 56.4 %psum.179 = bf16[16,512]{1,0:T(8,128)(2,1)S(1)} all-reduce(f32[16,512]{1,0:T(8,128)S(1)} %convolution_multiply_fusion.27), channel_id=1, replica_groups=mesh['neuron'=16,'trial'=8] {'neuron'}, use_global_device_ids=true, to_apply=%region_4.0 | all-reduce | flops 8192 | bytes 49152 | tf_op jit(solution)/shard_map/psum | solution.py:44
  343.6 7.0 bitcast_dynamic-update-slice_fusion.4
  355.2 55.7 %psum.180 = bf16[16,512]{1,0:T(8,128)(2,1)S(1)} all-reduce(f32[16,512]{1,0:T(8,128)S(1)} %convolution_multiply_fusion.26), channel_id=1, replica_groups=mesh['neuron'=16,'trial'=8] {'neuron'}, use_global_device_ids=true, to_apply=%region_5.0 | all-reduce | flops 8192 | bytes 49152 | tf_op jit(solution)/shard_map/psum | solution.py:44
  410.9 7.4 bitcast_dynamic-update-slice_fusion.3
  425.3 56.5 %psum.181 = bf16[16,512]{1,0:T(8,128)(2,1)S(1)} all-reduce(f32[16,512]{1,0:T(8,128)} %convolution_multiply_fusion.25), channel_id=1, replica_groups=mesh['neuron'=16,'trial'=8] {'neuron'}, use_global_device_ids=true, to_apply=%region_6.0 | all-reduce | flops 8192 | bytes 49152 | tf_op jit(solution)/shard_map/psum | solution.py:44
  481.7 7.4 bitcast_dynamic-update-slice_fusion.2
  516.7 55.9 %psum.182 = bf16[16,512]{1,0:T(8,128)(2,1)S(1)} all-reduce(f32[16,512]{1,0:T(8,128)S(1)} %copy-done.39), channel_id=1, replica_groups=mesh['neuron'=16,'trial'=8] {'neuron'}, use_global_device_ids=true, to_apply=%region_7.0 | all-reduce | flops 8192 | bytes 49152 | tf_op jit(solution)/shard_map/psum | solution.py:44
  593.8 61.6 %all-reduce.6 = (bf16[16,512]{1,0:T(8,128)(2,1)S(1)}, bf16[16,512]{1,0:T(8,128)(2,1)S(1)}, bf16[16,512]{1,0:T(8,128)(2,1)S(1)}, bf16[16,512]{1,0:T(8,128)(2,1)S(...) all-reduce(f32[16,512]{1,0:T(8,128)S(1)} %convolution_multiply_fusi, ...), channel_id=1, replica_groups=mesh['neuron'=16,'trial'=8] {'neuron'}, use_global_device_ids=true, to_apply=%region_8.0 | all-reduce | flops 131072 | bytes 786432 | tf_op jit(solution)/shard_map/psum | solution.py:67
  656.1 13.1 %copy.34 = bf16[8,16,8192]{1,0,2:T(8,128)(2,1)} copy(bf16[8,16,8192]{2,1,0:T(8,128)(2,1)S(1)} %copy-done.19) | data formatting | bytes 4194304 | tf_op jit(solution)/shard_map/stack | solution.py:71
  669.3 19.6 %reshape.114 = bf16[8,2,65536]{2,1,0:T(2,128)(2,1)} reshape(bf16[8192,8,16]{2,1,0:T(8,128)(2,1)} %bitcast.266) | data formatting | bytes 4194304
  688.8 128.3 %all-to-all-start.1 = ((bf16[8,2,65536]{2,1,0:T(2,128)(2,1)}), bf16[8,2,65536]{2,1,0:T(2,128)(2,1)S(1)}, u32[]{:S(2)}, u32[]{:S(2)}) async-start(bf16[8,2,65536]{2,1,0:T(2,128)(2,1)} %reshape.114), calls=%async_computation.1 | async-start | bytes 4194304 | tf_op jit(solution)/shard_map/all_to_all | solution.py:81
  819.8 14.5 %copy.30 = bf16[8,16,8192]{1,0,2:T(8,128)(2,1)} copy(bf16[8,16,8192]{2,1,0:T(8,128)(2,1)} %bitcast_dynamic-update-slice_fusion.9) | data formatting | bytes 4194304 | tf_op jit(solution)/shard_map/stack | solution.py:70
  834.4 19.6 %reshape.112 = bf16[8,2,65536]{2,1,0:T(2,128)(2,1)} reshape(bf16[8192,8,16]{2,1,0:T(8,128)(2,1)} %bitcast.267) | data formatting | bytes 4194304
  858.7 13.1 %reshape.115 = bf16[8192,8,16]{2,1,0:T(8,128)(2,1)} reshape(bf16[8,2,65536]{2,1,0:T(2,128)(2,1)S(1)} %all-to-all-done.1) | data formatting | bytes 4194304
  871.8 17.1 %copy.36 = bf16[8,8,16,1024]{3,2,1,0:T(8,128)(2,1)} copy(bf16[8,8,16,1024]{2,0,3,1:T(8,128)(2,1)} %bitcast.268) | data formatting | bytes 4194304 | tf_op jit(solution)/shard_map/all_to_all | solution.py:81
  896.9 13.9 %reshape.113 = bf16[8192,8,16]{2,1,0:T(8,128)(2,1)} reshape(bf16[8,2,65536]{2,1,0:T(2,128)(2,1)} %all-to-all-done) | data formatting | bytes 4194304
  910.8 17.5 %copy.32 = bf16[8,8,16,1024]{3,2,1,0:T(8,128)(2,1)} copy(bf16[8,8,16,1024]{2,0,3,1:T(8,128)(2,1)} %bitcast.269) | data formatting | bytes 4194304 | tf_op jit(solution)/shard_map/all_to_all | solution.py:80
  932.8 109.1 %all-reduce.5.cloned.1.call-done = f32[512,512]{0,1:T(8,128)} async-done(((f32[512,512]{0,1:T(8,128)}), f32[512,512]{0,1:T(8,128)}) %all-reduce.5.cloned.1.call-update) | async-done | bytes 1048592 | tf_op jit(solution)/shard_map/psum | solution.py:99
  1047.0 11.7 cholesky.104
  1058.9 9.8 custom-call.30
  1071.2 11.7 cholesky.217
  1083.0 9.9 custom-call.31
  1094.5 11.7 cholesky.238
  1106.9 9.8 custom-call.32
  1118.1 11.9 cholesky.255
  1135.0 13.6 %while.1 = (s32[]{:T(128)}, f32[512,512]{1,0:T(8,128)}, s32[4,2]{0,1:T(2,128)S(1)}, f32[4,128,128]{2,1,0:T(8,128)}, s32[]{:T(128)}) while((s32[]{:T(128)}, f32[512,512]{1,0:T(8,128)}, s32[4,2]{0,1:T(2,128)S(1)}, f32[4,128,128]{2,1,0:T(8,128)}, s32[]{:T(128)}) %tuple.66), condition=%wide.while_cond, body=%wide.while_body.sunk | while | flops 2 | bytes 132705 | solution.py:103
  1148.7 40.1 %custom-call.33 = f32[4,128,128]{1,2,0:T(8,128)S(1)} custom-call(f32[4,128,128]{2,1,0:T(8,128)} %get-tuple-element.9), custom_call_target="InvertDiagBlocksLowerTriangular" | custom-call | tf_op jit(solution)/shard_map/triangular_solve | solution.py:103
  (201 shorter events, 169.8 us)
Async XLA Ops:
  7.2 67.7 %copy-start.11 = (f32[16,8192]{1,0:T(8,128)S(1)}, f32[16,8192]{1,0:T(8,128)}, u32[]{:S(2)}) copy-start(f32[16,8192]{1,0:T(8,128)} %param.13) | copy-start | bytes 1572868
  7.2 67.7 %copy-start.10 = (f32[16,8192]{1,0:T(8,128)S(1)}, f32[16,8192]{1,0:T(8,128)}, u32[]{:S(2)}) copy-start(f32[16,8192]{1,0:T(8,128)} %param.14) | copy-start | bytes 1572868
  7.2 67.7 %copy-start.17 = (f32[8192]{0:T(1024)S(1)}, f32[8192]{0:T(1024)}, u32[]{:S(2)}) copy-start(f32[8192]{0:T(1024)} %param.18) | copy-start | bytes 98308
  7.2 67.6 %copy-start.18 = (f32[8192]{0:T(1024)S(1)}, f32[8192]{0:T(1024)}, u32[]{:S(2)}) copy-start(f32[8192]{0:T(1024)} %param.19) | copy-start | bytes 98308
  7.2 67.6 %copy-start.25 = (f32[16,8192]{1,0:T(8,128)S(1)}, f32[16,8192]{1,0:T(8,128)}, u32[]{:S(2)}) copy-start(f32[16,8192]{1,0:T(8,128)} %param.15) | copy-start | bytes 1572868
  7.2 67.6 %copy-start.23 = (f32[8192]{0:T(1024)S(1)}, f32[8192]{0:T(1024)}, u32[]{:S(2)}) copy-start(f32[8192]{0:T(1024)} %param.16) | copy-start | bytes 98308
  7.2 67.6 %copy-start.24 = (f32[8192]{0:T(1024)S(1)}, f32[8192]{0:T(1024)}, u32[]{:S(2)}) copy-start(f32[8192]{0:T(1024)} %param.17) | copy-start | bytes 98308
  7.2 881.6 %all-gather.5.cloned.1.call-start = ((), (), s32[]{:S(2)}) async-start(), calls=%async_computation.3 | async-start | bytes 1179648 | tf_op jit(solution)/shard_map/all_gather | solution.py:91
  74.9 6.7 copy-start
  145.7 60.9 %copy-start.13 = (f32[16,8192]{1,0:T(8,128)}, f32[16,8192]{1,0:T(8,128)S(1)}, u32[]{:S(2)}) copy-start(f32[16,8192]{1,0:T(8,128)S(1)} %get-tuple-element.64) | copy-start | bytes 1572868
  145.7 128.1 %copy-start.2 = (f32[16,8192]{1,0:T(8,128)}, f32[16,8192]{1,0:T(8,128)S(1)}, u32[]{:S(2)}) copy-start(f32[16,8192]{1,0:T(8,128)S(1)} %get-tuple-element.62) | copy-start | bytes 1572868
  145.7 60.9 %copy-start.26 = (f32[16,8192]{1,0:T(8,128)S(1)}, f32[16,8192]{1,0:T(8,128)}, u32[]{:S(2)}) copy-start(f32[16,8192]{1,0:T(8,128)} %get-tuple-element.86) | copy-start | bytes 1572868
  213.3 60.5 %copy-start.14 = (f32[16,8192]{1,0:T(8,128)S(1)}, f32[16,8192]{1,0:T(8,128)}, u32[]{:S(2)}) copy-start(f32[16,8192]{1,0:T(8,128)} %copy-done.13) | copy-start | bytes 1572868
  282.6 61.0 %copy-start.4 = (f32[16,8192]{1,0:T(8,128)S(1)}, f32[16,8192]{1,0:T(8,128)}, u32[]{:S(2)}) copy-start(f32[16,8192]{1,0:T(8,128)} %get-tuple-element.55) | copy-start | bytes 1572868
  481.7 18.2 %slice-start.4 = ((s8[8388608]{0:T(1024)(128)(4,1)}), s8[4194304]{0:T(1024)(128)(4,1)S(1)}, s32[]{:S(2)}) async-start(s8[8388608]{0:T(1024)(128)(4,1)} %bitcast.264), calls=%async_computation.9 | async-start | bytes 8388608
  489.1 5.4 copy-start.8
  489.1 5.4 copy-start.1
  489.1 10.8 slice-start.5
  494.5 7.2 slice-start
  499.9 2.3 copy-start.6
  514.9 57.8 %copy-start.7 = (f32[16,8192]{1,0:T(8,128)S(1)}, f32[16,8192]{1,0:T(8,128)}, u32[]{:S(2)}) copy-start(f32[16,8192]{1,0:T(8,128)} %get-tuple-element.48) | copy-start | bytes 1572868
  514.9 57.8 %copy-start.9 = (f32[16,8192]{1,0:T(8,128)S(1)}, f32[16,8192]{1,0:T(8,128)}, u32[]{:S(2)}) copy-start(f32[16,8192]{1,0:T(8,128)} %copy-done.8) | copy-start | bytes 1572868
  514.9 57.8 %copy-start.12 = (f32[16,8192]{1,0:T(8,128)S(1)}, f32[16,8192]{1,0:T(8,128)}, u32[]{:S(2)}) copy-start(f32[16,8192]{1,0:T(8,128)} %get-tuple-element.50) | copy-start | bytes 1572868
  579.3 9.5 slice-start.2
  584.0 4.7 slice-start.3
  584.1 4.7 copy-start.22
  592.5 63.6 %copy-start.19 = (bf16[8,16,8192]{2,1,0:T(8,128)(2,1)S(1)}, bf16[8,16,8192]{2,1,0:T(8,128)(2,1)}, u32[]{:S(2)}) copy-start(bf16[8,16,8192]{2,1,0:T(8,128)(2,1)} %get-tuple-element.42) | copy-start | bytes 6291460
  688.8 165.1 %all-to-all-start.1 = ((bf16[8,2,65536]{2,1,0:T(2,128)(2,1)}), bf16[8,2,65536]{2,1,0:T(2,128)(2,1)S(1)}, u32[]{:S(2)}, u32[]{:S(2)}) async-start(bf16[8,2,65536]{2,1,0:T(2,128)(2,1)} %reshape.114), calls=%async_computation.1 | async-start | bytes 4194304 | tf_op jit(solution)/shard_map/all_to_all | solution.py:81
  817.1 111.2 %all-gather.3.cloned.1.call-start = ((), (), s32[]{:S(2)}) async-start(), calls=%async_computation.2 | async-start | bytes 1179648 | tf_op jit(solution)/shard_map/all_gather | solution.py:85
  853.9 42.9 %all-to-all-start = ((bf16[8,2,65536]{2,1,0:T(2,128)(2,1)}), bf16[8,2,65536]{2,1,0:T(2,128)(2,1)}, u32[]{:S(2)}, u32[]{:S(2)}) async-start(bf16[8,2,65536]{2,1,0:T(2,128)(2,1)} %reshape.112), calls=%async_computation | async-start | bytes 4194304 | tf_op jit(solution)/shard_map/all_to_all | solution.py:80
  858.7 183.2 %all-reduce.5.cloned.1.call-start = ((), (), s32[]{:S(2)}) async-start(), calls=%async_computation.4 | async-start | bytes 2097152 | tf_op jit(solution)/shard_map/psum | solution.py:99
  1041.9 2.6 copy-start.15
  (19 other events, 25.3 us)
Sparse Core Ops, SparseCore 0:
  656.3 144.7 all-gather.4
  819.6 23.4 all-gather.2
  897.0 144.9 all-reduce.4
where the time goes:
time: 1230 us; the launch traced here: 1210 us
  blocking collectives  516 us (42%)
  matrix products  162 us (13%)
  local copies, waits for them, and re-layouts  149 us (12%)
  starting transfers between devices  133 us (11%)
  other arithmetic  127 us (10%)
  waiting for transfers between devices  109 us (9%)
  between operations  17.4 us (1%)
    psum x8, blocking collectives, shards(): projected = lax.psum(partial_value, 'neuron').astype(jnp.bfloat16)  455 us
    all_to_all x1, starting transfers between devices, shards(): lax.all_to_all(presyn_all, 'trial', split_axis=2, concat_axis=1, tiled=True)  128 us
    psum x1, waiting for transfers between devices, shards(): lax.psum(lax.dot_general(right_step, right_step, row_lead, precision=high...  109 us
    another operation x14, other arithmetic, shards(): lower_one = jnp.linalg.cholesky(gram_one)  78.7 us
    dot_general x24, matrix products, rank_block(): return jnp.dot(values, factor, preferred_element_type=jnp.float32) * weight  71.5 us
    unnamed x111, local copies, waits for them, and re-layouts  70.7 us
    psum x1, blocking collectives, shards(): g_total, k_total = lax.psum((g_part, k_part), 'neuron')  61.6 us
    dot_general x8, matrix products, shards(): lax.dot_general(projected, left_factor, (((1,), (1,)), ((), ())), preferr...  55.8 us
  transfers between devices with their start and end apart: 5, of which 1 were waited for; matrix products, arithmetic and copies ran while one was open for 12% of the time, Pallas kernels for 0%

commit v1 on v0

--- a/solution.py
+++ b/solution.py
@@ -78,7 +78,12 @@
     contract_lead = (((0, 1), (0, 1)), ((), ()))
     signal_mine, presyn_mine = (
         lax.all_to_all(signal_all, "trial", split_axis=2, concat_axis=1, tiled=True),
-        lax.all_to_all(presyn_all, "trial", split_axis=2, concat_axis=1, tiled=True),
+        jnp.concatenate(
+            lax.all_to_all(
+                jnp.stack(jnp.split(presyn_all, lax.axis_size("trial"), axis=2)), "trial", 0, 0
+            ),
+            axis=1,
+        ),
     )
     first = lax.dot_general(
         signal_mine,

time: 1230 us -> 1190 us (0.967)
  local copies, waits for them, and re-layouts: 149 us -> 99.6 us
  matrix products: 162 us -> 176 us
    unnamed x111 -> x120, local copies, waits for them, and re-layouts: 70.7 us -> 46.5 us
    all_to_all x1 -> x0, local copies, waits for them, and re-layouts: 17.1 us -> none  [shards(): lax.all_to_all(presyn_all, 'trial', split_axis=2, concat_axis=1, tiled=True)]
    all_to_all x1, waiting for transfers between devices: 0.01 us -> 15.7 us  [shards(): lax.all_to_all(signal_all, 'trial', split_axis=2, concat_axis=1, tiled=True)]
    dot_general x24, matrix products: 71.5 us -> 86.7 us  [rank_block(): return jnp.dot(values, factor, preferred_element_type=jnp.float32) * weight]
    psum x1, waiting for transfers between devices: 109 us -> 96 us  [shards(): lax.psum(lax.dot_general(right_step, right_step, row_lead, precision=high...]
  transfers between devices with their start and end apart: 5 -> 5, of which waited for: 1 -> 2; matrix products, arithmetic and copies ran while one was open for 12% -> 8% of each run, Pallas kernels for 0% -> 0%
where the time goes in v1:
time: 1190 us; the launch traced here: 1180 us
  blocking collectives  514 us (43%)
  matrix products  176 us (15%)
  starting transfers between devices  135 us (11%)
  other arithmetic  126 us (11%)
  waiting for transfers between devices  112 us (9%)
  local copies, waits for them, and re-layouts  99.6 us (8%)
  between operations  17.4 us (1%)
    psum x8, blocking collectives, shards(): projected = lax.psum(partial_value, 'neuron').astype(jnp.bfloat16)  453 us
    all_to_all x1, starting transfers between devices, shards(): lax.all_to_all(jnp.stack(jnp.split(presyn_all, lax.axis_size('trial'), ax...  130 us
    psum x1, waiting for transfers between devices, shards(): lax.psum(lax.dot_general(right_step, right_step, row_lead, precision=high...  96 us
    dot_general x24, matrix products, rank_block(): return jnp.dot(values, factor, preferred_element_type=jnp.float32) * weight  86.7 us
    another operation x14, other arithmetic, shards(): lower_one = jnp.linalg.cholesky(gram_one)  79.1 us
    psum x1, blocking collectives, shards(): g_total, k_total = lax.psum((g_part, k_part), 'neuron')  61.3 us
    dot_general x8, matrix products, shards(): lax.dot_general(projected, left_factor, (((1,), (1,)), ((), ())), preferr...  54.6 us
    unnamed x120, local copies, waits for them, and re-layouts  46.5 us
  transfers between devices with their start and end apart: 5, of which 2 were waited for; matrix products, arithmetic and copies ran while one was open for 8% of the time, Pallas kernels for 0%

profile of v1, /device:TPU:1, one launch (start us, length us, event | category | flops | bytes accessed | tf_op | source)
XLA Modules:
  0.0 1180.8 jit_solution(11981548736725691954)
XLA Ops:
  12.3 62.5 %psum.175 = bf16[16,512]{1,0:T(8,128)(2,1)S(1)} all-reduce(f32[16,512]{1,0:T(8,128)S(1)} %convolution_multiply_fusion.31), channel_id=1, replica_groups=mesh['neuron'=16,'trial'=8] {'neuron'}, use_global_device_ids=true, to_apply=%region_0.0 | all-reduce | flops 8192 | bytes 49152 | tf_op jit(solution)/shard_map/psum | solution.py:44
  74.9 6.7 bitcast_dynamic-update-slice_fusion.8
  82.8 55.9 %psum.176 = bf16[16,512]{1,0:T(8,128)(2,1)S(1)} all-reduce(f32[16,512]{1,0:T(8,128)S(1)} %convolution_multiply_fusion.30), channel_id=1, replica_groups=mesh['neuron'=16,'trial'=8] {'neuron'}, use_global_device_ids=true, to_apply=%region_1.0 | all-reduce | flops 8192 | bytes 49152 | tf_op jit(solution)/shard_map/psum | solution.py:44
  144.1 7.0 bitcast_dynamic-update-slice_fusion.7
  156.9 55.6 %psum.177 = bf16[16,512]{1,0:T(8,128)(2,1)S(1)} all-reduce(f32[16,512]{1,0:T(8,128)S(1)} %convolution_multiply_fusion.29), channel_id=1, replica_groups=mesh['neuron'=16,'trial'=8] {'neuron'}, use_global_device_ids=true, to_apply=%region_2.0 | all-reduce | flops 8192 | bytes 49152 | tf_op jit(solution)/shard_map/psum | solution.py:44
  212.5 6.6 bitcast_dynamic-update-slice_fusion.6
  229.0 56.0 %psum.178 = bf16[16,512]{1,0:T(8,128)(2,1)S(1)} all-reduce(f32[16,512]{1,0:T(8,128)S(1)} %convolution_multiply_fusion.28), channel_id=1, replica_groups=mesh['neuron'=16,'trial'=8] {'neuron'}, use_global_device_ids=true, to_apply=%region_3.0 | all-reduce | flops 8192 | bytes 49152 | tf_op jit(solution)/shard_map/psum | solution.py:44
  285.0 7.0 bitcast_dynamic-update-slice_fusion.5
  304.1 55.6 %psum.179 = bf16[16,512]{1,0:T(8,128)(2,1)S(1)} all-reduce(f32[16,512]{1,0:T(8,128)S(1)} %convolution_multiply_fusion.27), channel_id=1, replica_groups=mesh['neuron'=16,'trial'=8] {'neuron'}, use_global_device_ids=true, to_apply=%region_4.0 | all-reduce | flops 8192 | bytes 49152 | tf_op jit(solution)/shard_map/psum | solution.py:44
  376.2 55.7 %psum.180 = bf16[16,512]{1,0:T(8,128)(2,1)S(1)} all-reduce(f32[16,512]{1,0:T(8,128)S(1)} %convolution_multiply_fusion.26), channel_id=1, replica_groups=mesh['neuron'=16,'trial'=8] {'neuron'}, use_global_device_ids=true, to_apply=%region_5.0 | all-reduce | flops 8192 | bytes 49152 | tf_op jit(solution)/shard_map/psum | solution.py:44
  433.6 7.0 bitcast_dynamic-update-slice_fusion.3
  452.7 56.0 %psum.181 = bf16[16,512]{1,0:T(8,128)(2,1)S(1)} all-reduce(f32[16,512]{1,0:T(8,128)S(1)} %convolution_multiply_fusion.25), channel_id=1, replica_groups=mesh['neuron'=16,'trial'=8] {'neuron'}, use_global_device_ids=true, to_apply=%region_6.0 | all-reduce | flops 8192 | bytes 49152 | tf_op jit(solution)/shard_map/psum | solution.py:44
  510.5 6.7 bitcast_dynamic-update-slice_fusion.2
  533.4 55.7 %psum.182 = bf16[16,512]{1,0:T(8,128)(2,1)S(1)} all-reduce(f32[16,512]{1,0:T(8,128)S(1)} %copy-done.37), channel_id=1, replica_groups=mesh['neuron'=16,'trial'=8] {'neuron'}, use_global_device_ids=true, to_apply=%region_7.0 | all-reduce | flops 8192 | bytes 49152 | tf_op jit(solution)/shard_map/psum | solution.py:44
  589.2 6.8 bitcast_dynamic-update-slice_fusion.1
  605.6 61.3 %all-reduce.6 = (bf16[16,512]{1,0:T(8,128)(2,1)S(1)}, bf16[16,512]{1,0:T(8,128)(2,1)S(1)}, bf16[16,512]{1,0:T(8,128)(2,1)S(1)}, bf16[16,512]{1,0:T(8,128)(2,1)S(...) all-reduce(f32[16,512]{1,0:T(8,128)S(1)} %copy-done.36, ...), channel_id=1, replica_groups=mesh['neuron'=16,'trial'=8] {'neuron'}, use_global_device_ids=true, to_apply=%region_8.0 | all-reduce | flops 131072 | bytes 786432 | tf_op jit(solution)/shard_map/psum | solution.py:67
  677.5 129.9 %all-to-all-start.1 = ((bf16[8,8,16,1024]{3,2,1,0:T(8,128)(2,1)}), bf16[8,8,16,1024]{3,2,1,0:T(8,128)(2,1)}, u32[]{:S(2)}, u32[]{:S(2)}) async-start(bf16[8,8,16,1024]{3,2,1,0:T(8,128)(2,1)} %fusion.61), calls=%async_computation.1 | async-start | bytes 4194304 | tf_op jit(solution)/shard_map/all_to_all | solution.py:82
  809.3 14.5 %copy.29 = bf16[8,16,8192]{1,0,2:T(8,128)(2,1)} copy(bf16[8,16,8192]{2,1,0:T(8,128)(2,1)} %bitcast_dynamic-update-slice_fusion.9) | data formatting | bytes 4194304 | tf_op jit(solution)/shard_map/stack | solution.py:70
  823.9 19.6 %reshape.120 = bf16[8,2,65536]{2,1,0:T(2,128)(2,1)} reshape(bf16[8192,8,16]{2,1,0:T(8,128)(2,1)} %bitcast.297) | data formatting | bytes 4194304
  859.5 15.7 %all-to-all-done = bf16[8,2,65536]{2,1,0:T(2,128)(2,1)} async-done(((bf16[8,2,65536]{2,1,0:T(2,128)(2,1)}), bf16[8,2,65536]{2,1,0:T(2,128)(2,1)}, u32[]{:S(2)}, u32[]{:S(2)}) %all-to-all-start) | async-done | bytes 2097184 | tf_op jit(solution)/shard_map/all_to_all | solution.py:80
  875.2 13.9 %reshape.121 = bf16[8192,8,16]{2,1,0:T(8,128)(2,1)} reshape(bf16[8,2,65536]{2,1,0:T(2,128)(2,1)} %all-to-all-done) | data formatting | bytes 4194304
  889.1 17.2 %copy.31 = bf16[8,8,16,1024]{3,2,1,0:T(8,128)(2,1)} copy(bf16[8,8,16,1024]{2,0,3,1:T(8,128)(2,1)} %bitcast.298) | data formatting | bytes 4194304 | tf_op jit(solution)/shard_map/all_to_all | solution.py:80
  910.9 96.0 %all-reduce.5.cloned.1.call-done = f32[512,512]{0,1:T(8,128)} async-done(((f32[512,512]{0,1:T(8,128)}), f32[512,512]{0,1:T(8,128)}) %all-reduce.5.cloned.1.call-update) | async-done | bytes 1048592 | tf_op jit(solution)/shard_map/psum | solution.py:104
  1011.9 11.7 cholesky.104
  1023.6 9.8 custom-call.30
  1036.1 11.7 cholesky.217
  1047.8 10.0 custom-call.31
  1059.4 11.7 cholesky.238
  1071.8 9.8 custom-call.32
  1083.1 12.1 %cholesky.255 = f32[128,128]{1,0:T(8,128)S(1)} custom-call(f32[128,128]{1,0:T(8,128)S(1)} %convolution_subtract_fusion.4), custom_call_target="Cholesky" | custom-call | tf_op jit(solution)/shard_map/jit(cholesky)/cholesky | solution.py:107
  1100.5 14.6 %while.1 = (s32[]{:T(128)}, f32[512,512]{1,0:T(8,128)}, s32[4,2]{0,1:T(2,128)S(1)}, f32[4,128,128]{2,1,0:T(8,128)}, s32[]{:T(128)}) while((s32[]{:T(128)}, f32[512,512]{1,0:T(8,128)}, s32[4,2]{0,1:T(2,128)S(1)}, f32[4,128,128]{2,1,0:T(8,128)}, s32[]{:T(128)}) %tuple.66), condition=%wide.while_cond, body=%wide.while_body.sunk | while | flops 2 | bytes 132205 | solution.py:108
  1115.1 40.1 %custom-call.33 = f32[4,128,128]{1,2,0:T(8,128)S(1)} custom-call(f32[4,128,128]{2,1,0:T(8,128)} %get-tuple-element.9), custom_call_target="InvertDiagBlocksLowerTriangular" | custom-call | tf_op jit(solution)/shard_map/triangular_solve | solution.py:108
  (212 shorter events, 177.4 us)
Async XLA Ops:
  7.2 67.7 %copy-start.13 = (f32[8192]{0:T(1024)S(1)}, f32[8192]{0:T(1024)}, u32[]{:S(2)}) copy-start(f32[8192]{0:T(1024)} %param.19) | copy-start | bytes 98308
  7.2 67.7 %copy-start.12 = (f32[8192]{0:T(1024)S(1)}, f32[8192]{0:T(1024)}, u32[]{:S(2)}) copy-start(f32[8192]{0:T(1024)} %param.18) | copy-start | bytes 98308
  7.2 67.7 %copy-start.3 = (f32[16,8192]{1,0:T(8,128)S(1)}, f32[16,8192]{1,0:T(8,128)}, u32[]{:S(2)}) copy-start(f32[16,8192]{1,0:T(8,128)} %param.14) | copy-start | bytes 1572868
  7.2 67.7 %copy-start.4 = (f32[16,8192]{1,0:T(8,128)S(1)}, f32[16,8192]{1,0:T(8,128)}, u32[]{:S(2)}) copy-start(f32[16,8192]{1,0:T(8,128)} %param.13) | copy-start | bytes 1572868
  7.2 67.7 %copy-start.18 = (f32[8192]{0:T(1024)S(1)}, f32[8192]{0:T(1024)}, u32[]{:S(2)}) copy-start(f32[8192]{0:T(1024)} %param.17) | copy-start | bytes 98308
  7.2 67.7 %copy-start.17 = (f32[8192]{0:T(1024)S(1)}, f32[8192]{0:T(1024)}, u32[]{:S(2)}) copy-start(f32[8192]{0:T(1024)} %param.16) | copy-start | bytes 98308
  7.2 67.7 %copy-start.19 = (f32[16,8192]{1,0:T(8,128)S(1)}, f32[16,8192]{1,0:T(8,128)}, u32[]{:S(2)}) copy-start(f32[16,8192]{1,0:T(8,128)} %param.15) | copy-start | bytes 1572868
  7.2 844.3 %all-gather.5.cloned.1.call-start = ((), (), s32[]{:S(2)}) async-start(), calls=%async_computation.3 | async-start | bytes 1179648 | tf_op jit(solution)/shard_map/all_gather | solution.py:96
  74.9 6.7 copy-start
  138.7 12.5 %slice-start = ((s8[8388608]{0:T(1024)(128)(4,1)}), s8[4194304]{0:T(1024)(128)(4,1)S(1)}, s32[]{:S(2)}) async-start(s8[8388608]{0:T(1024)(128)(4,1)} %bitcast.287), calls=%async_computation.5 | async-start | bytes 8388608
  138.7 13.7 %slice-start.8 = ((s8[8388608]{0:T(1024)(128)(4,1)}), s8[4194304]{0:T(1024)(128)(4,1)S(1)}, s32[]{:S(2)}) async-start(s8[8388608]{0:T(1024)(128)(4,1)} %bitcast.295), calls=%async_computation.13 | async-start | bytes 8388608
  144.1 7.0 slice-start.1
  144.1 8.2 slice-start.9
  151.1 61.4 %copy-start.7 = (f32[16,8192]{1,0:T(8,128)}, f32[16,8192]{1,0:T(8,128)S(1)}, u32[]{:S(2)}) copy-start(f32[16,8192]{1,0:T(8,128)S(1)} %get-tuple-element.64) | copy-start | bytes 1572868
  155.1 57.4 %copy-start.23 = (f32[16,8192]{1,0:T(8,128)S(1)}, f32[16,8192]{1,0:T(8,128)}, u32[]{:S(2)}) copy-start(f32[16,8192]{1,0:T(8,128)} %get-tuple-element.86) | copy-start | bytes 1572868
  292.0 67.7 %copy-start.6 = (f32[16,8192]{1,0:T(8,128)}, f32[16,8192]{1,0:T(8,128)S(1)}, u32[]{:S(2)}) copy-start(f32[16,8192]{1,0:T(8,128)S(1)} %get-tuple-element.57) | copy-start | bytes 1572868
  292.0 10.2 slice-start.2
  296.8 5.4 slice-start.3
  302.3 57.4 %copy-start.22 = (f32[16,8192]{1,0:T(8,128)S(1)}, f32[16,8192]{1,0:T(8,128)}, u32[]{:S(2)}) copy-start(f32[16,8192]{1,0:T(8,128)} %get-tuple-element.88) | copy-start | bytes 1572868
  440.7 69.8 %copy-start.5 = (f32[16,8192]{1,0:T(8,128)}, f32[16,8192]{1,0:T(8,128)S(1)}, u32[]{:S(2)}) copy-start(f32[16,8192]{1,0:T(8,128)S(1)} %get-tuple-element.50) | copy-start | bytes 1572868
  440.7 10.2 slice-start.4
  445.5 5.4 slice-start.5
  450.9 59.6 %copy-start.21 = (f32[16,8192]{1,0:T(8,128)S(1)}, f32[16,8192]{1,0:T(8,128)}, u32[]{:S(2)}) copy-start(f32[16,8192]{1,0:T(8,128)} %get-tuple-element.90) | copy-start | bytes 1572868
  517.2 5.4 copy-start.2
  517.2 5.4 copy-start.1
  517.2 10.8 slice-start.6
  667.7 6.9 copy-start.14
  677.5 131.1 %copy-start.9 = (f32[16,8192]{1,0:T(8,128)S(1)}, f32[16,8192]{1,0:T(8,128)}, u32[]{:S(2)}) copy-start(f32[16,8192]{1,0:T(8,128)} %copy-done.8) | copy-start | bytes 1572868
  677.5 166.0 %all-to-all-start.1 = ((bf16[8,8,16,1024]{3,2,1,0:T(8,128)(2,1)}), bf16[8,8,16,1024]{3,2,1,0:T(8,128)(2,1)}, u32[]{:S(2)}, u32[]{:S(2)}) async-start(bf16[8,8,16,1024]{3,2,1,0:T(8,128)(2,1)} %fusion.61), calls=%async_computation.1 | async-start | bytes 4194304 | tf_op jit(solution)/shard_map/all_to_all | solution.py:82
  807.4 99.0 %all-gather.3.cloned.1.call-start = ((), (), s32[]{:S(2)}) async-start(), calls=%async_computation.2 | async-start | bytes 1179648 | tf_op jit(solution)/shard_map/all_gather | solution.py:90
  843.5 31.8 %all-to-all-start = ((bf16[8,2,65536]{2,1,0:T(2,128)(2,1)}), bf16[8,2,65536]{2,1,0:T(2,128)(2,1)}, u32[]{:S(2)}, u32[]{:S(2)}) async-start(bf16[8,2,65536]{2,1,0:T(2,128)(2,1)} %reshape.120), calls=%async_computation | async-start | bytes 4194304 | tf_op jit(solution)/shard_map/all_to_all | solution.py:80
  848.2 158.6 %all-reduce.5.cloned.1.call-start = ((), (), s32[]{:S(2)}) async-start(), calls=%async_computation.4 | async-start | bytes 2097152 | tf_op jit(solution)/shard_map/psum | solution.py:104
  (21 other events, 76.9 us)
Sparse Core Ops, SparseCore 0:
  667.8 149.1 all-gather.4
  818.7 25.6 all-gather.2
  859.6 147.1 all-reduce.4
